TPU v7x, 32 devices: a whole 2x2x4 slice. The times are simulated.
32 devices in a mesh: seq: 2 (over x), hist: 8 (over z, y), chan: 2 (over core).
Axes of the slice: x: 2, y: 2, z: 4, core: 2. Of those that a mesh axis runs over, the one named last changes fastest.
Arguments:
- history: bfloat16 [4096, 4096], P(('seq', 'hist'), 'chan'), parts along dimension 0, may hold values from -6 to 6
- filter_taps: bfloat16 [2048, 4096], P('hist', 'chan'), may hold values from -0.125 to 0.125
- gate_values: bfloat16 [512, 4096], P(('seq', 'hist'), 'chan'), parts along dimension 0, may hold values from -6 to 6
- out_weight: bfloat16 [4096, 4096], P('chan', 'hist'), may hold values from -0.09375 to 0.09375
Outputs:
- output: bfloat16 [512, 4096], P(('seq', 'hist', 'chan')), parts along dimension 0
There are 2 independent parts, one for each index of `seq`. A program takes and returns all parts, laid end to end along the dimension named above; an argument that names none is the same for every part. Nothing has to cross between parts.
All inputs are finite; a program needn't handle non-finite values.
Results may differ from a plain program's by a relative error of at most 0.013.
Values may be sent and summed in bfloat16 or wider, within the bound.
A program may use at most 64 MiB of HBM per device.

v0:
```python
import math

import jax
import jax.numpy as jnp
from jax import lax
from jax.sharding import PartitionSpec as P


def shifted(value, axis, steps):
    count = lax.axis_size(axis)
    initial, last = (max(0, -steps), min(count, count - steps))
    return lax.ppermute(value, axis, [(source, source + steps) for source in range(initial, last)])


def split_product(table_high, table_low, values):
    first = jnp.dot(table_high, values, preferred_element_type=jnp.float32)
    return first + jnp.dot(table_low, values, preferred_element_type=jnp.float32)


def inverse_part(real_part, imag_part, block_tokens, period, row_count):
    scale = 2.0 * math.pi / period
    lags = block_tokens - 1 - lax.broadcasted_iota(jnp.int32, (row_count, period), 0)
    orders = lax.broadcasted_iota(jnp.int32, (row_count, period), 1)
    phases = (lags * orders % period).astype(jnp.float32) * scale
    cosines = jnp.dot(
        jnp.cos(phases),
        real_part,
        precision=lax.Precision.HIGHEST,
        preferred_element_type=jnp.float32,
    )
    sines = jnp.dot(
        jnp.sin(phases),
        imag_part,
        precision=lax.Precision.HIGHEST,
        preferred_element_type=jnp.float32,
    )
    return (cosines - sines) / period


def local(history, filter_taps, gate_values, out_weight):
    local_rows, channels = history.shape
    owned_rows = gate_values.shape[0]
    count_hist = lax.axis_size("hist")
    count_chan = lax.axis_size("chan")
    block_tokens = owned_rows * count_hist
    period = local_rows + block_tokens
    next_taps = shifted(filter_taps, "hist", -1)
    extended = jnp.concatenate([filter_taps, next_taps], 0)
    scale = 2.0 * math.pi / period
    modes = lax.broadcasted_iota(jnp.int32, (period, period), 0)
    places = lax.broadcasted_iota(jnp.int32, (period, period), 1)
    angles = (modes * places % period).astype(jnp.float32) * scale
    table = jnp.concatenate([jnp.cos(angles), jnp.sin(angles)], 0)
    table_high = table.astype(jnp.bfloat16)
    table_low = (table - table_high.astype(jnp.float32)).astype(jnp.bfloat16)
    spec_taps = split_product(table_high, table_low, extended)
    spec_input = split_product(table_high[:, :local_rows], table_low[:, :local_rows], history)
    taps_cos, taps_sin = (spec_taps[:period], spec_taps[period:])
    input_cos, input_sin = (spec_input[:period], spec_input[period:])
    real_part = taps_cos * input_cos + taps_sin * input_sin
    imag_part = taps_cos * input_sin - taps_sin * input_cos
    conv = lax.psum_scatter(
        inverse_part(
            real_part, imag_part, block_tokens, period, owned_rows * lax.axis_size("hist")
        ),
        "hist",
        scatter_dimension=0,
        tiled=True,
    )
    gated = (conv * gate_values.astype(jnp.float32)).astype(jnp.bfloat16)
    partial_value = jnp.dot(
        lax.all_gather(gated, "hist", axis=0, tiled=True),
        out_weight,
        preferred_element_type=jnp.float32,
    )
    columns = partial_value.shape[1]
    half_rows = owned_rows // count_chan
    ordered = partial_value.reshape(count_hist, count_chan, half_rows, columns).transpose(
        1, 0, 2, 3
    )
    ordered = ordered.reshape(count_chan * count_hist * half_rows, columns)
    summed = lax.psum_scatter(ordered.astype(jnp.bfloat16), "chan", scatter_dimension=0, tiled=True)
    output = lax.all_to_all(summed, "hist", split_axis=0, concat_axis=1, tiled=True)
    return output


def solution(mesh):
    return jax.shard_map(
        local,
        mesh=mesh,
        in_specs=(
            P(("seq", "hist"), "chan"),
            P("hist", "chan"),
            P(("seq", "hist"), "chan"),
            P("chan", "hist"),
        ),
        out_specs=P(("seq", "hist", "chan"), None),
        check_vma=False,
    )
```

profile of v0, /device:TPU:1, one launch (start us, length us, event | category | flops | bytes accessed | tf_op | source)
XLA Modules:
  0.0 192.9 jit_solution(3666349346221288854)
XLA Ops:
  6.5 1.5 collective-permute-start
  8.1 4.1 %fusion.36 = (f32[512,512]{1,0:T(8,128)S(1)}, f32[512,512]{1,0:T(8,128)S(1)}) fusion(), kind=kLoop, calls=%fused_computation.43 | loop fusion | flops 3670016 | bytes 2097152 | tf_op jit(solution)/shard_map/sin | solution.py:53
  12.2 0.3 subtract_convert_fusion
  12.5 0.1 fusion.22
  12.6 1.3 fusion.33
  13.9 0.1 constant_dynamic-update-slice_fusion.1
  14.0 1.4 convolution_add_fusion
  15.5 18.4 %collective-permute-done = bf16[256,2048]{1,0:T(8,128)(2,1)S(1)} collective-permute-done((bf16[256,2048]{1,0:T(8,128)(2,1)}, bf16[256,2048]{1,0:T(8,128)(2,1)S(1)}, u32[]{:S(2)}, u32[]{:S(2)}) %collective-permute-start) | collective-permute-done | bytes 1048608 | tf_op jit(solution)/shard_map/ppermute | solution.py:12
  33.8 0.1 constant_dynamic-update-slice_fusion
  33.9 2.4 %fusion.53 = f32[1024,2048]{1,0:T(8,128)S(1)} fusion(bf16[1024,512]{1,0:T(8,128)(2,1)S(1)} %subtract_convert_fusion, bf16[512,2048]{1,0:T(8,128)(2,1)S(1)} %constant_dynamic-update-slice_fusion), kind=kOutput, calls=%fused_computation.61 | convolution fusion | flops 2147483648 | bytes 11534336 | tf_op jit(solution)/shard_map/dot_general | solution.py:17
  36.3 2.4 %convolution_add_fusion.1 = f32[1024,2048]{1,0:T(8,128)S(1)} fusion(f32[1024,2048]{1,0:T(8,128)S(1)} %fusion.53, bf16[512,2048]{1,0:T(8,128)(2,1)S(1)} %constant_dynamic-update-slice_fusion, f32[512,512]{1,0:T(8,128)S(1)} %get-tuple-element.5, f32[512,512]{1,0:T(8,128)S(1)} %get-tuple-element.6), kind=kOutput, calls=%fused_computation.17 | convolution fusion | flops 2151677952 | bytes 20971520 | tf_op jit(solution)/shard_map/dot_general | solution.py:16
  38.7 6.2 %fusion = f32[256,2048]{1,0:T(8,128)S(1)} fusion(f32[1024,2048]{1,0:T(8,128)S(1)} %convolution_add_fusion, f32[1024,2048]{1,0:T(8,128)S(1)} %convolution_add_fusion.1, s32[256]{0:T(256)S(1)} %iota_subtract_fusion), kind=kOutput, calls=%fused_computation.1 | convolution fusion | flops 3226206208 | bytes 18875392 | tf_op jit(solution)/shard_map/dot_general | solution.py:31
  44.9 7.4 %fusion.19 = f32[256,2048]{1,0:T(8,128)} fusion(f32[256,2048]{1,0:T(8,128)S(1)} %fusion, f32[1024,2048]{1,0:T(8,128)S(1)} %convolution_add_fusion, f32[1024,2048]{1,0:T(8,128)S(1)} %convolution_add_fusion.1, s32[256]{0:T(256)S(1)} %iota_subtract_fusion), kind=kOutput, calls=%fused_computation.19 | convolution fusion | flops 3227254784 | bytes 20972544 | tf_op jit(solution)/shard_map/dot_general | solution.py:25
  52.4 0.0 reduce-scatter.3.cloned.1.call-update
  52.4 0.0 all-gather.2.cloned.1.call-start
  52.4 68.8 %reduce-scatter.3.cloned.1.call-done = f32[32,2048]{1,0:T(8,128)} async-done(((f32[256,2048]{1,0:T(8,128)}), f32[32,2048]{1,0:T(8,128)}) %reduce-scatter.3.cloned.1.call-update) | async-done | bytes 262160 | tf_op jit(solution)/shard_map/reduce_scatter | solution.py:62
  121.3 1.6 multiply_convert_fusion
  122.9 0.0 reduce-scatter.5.cloned.1.call-start
  123.0 39.6 %all-gather.2.cloned.1.call-done = bf16[256,2048]{1,0:T(8,128)(2,1)} async-done(((bf16[32,2048]{1,0:T(8,128)(2,1)}), bf16[256,2048]{1,0:T(8,128)(2,1)}) %all-gather.2.cloned.1.call-update) | async-done | bytes 1048592 | tf_op jit(solution)/shard_map/all_gather | solution.py:72
  162.5 1.9 convolution_convert_fusion
  164.5 0.7 copy.6
  165.2 8.7 %reduce-scatter.5.cloned.1.call-done = bf16[128,512]{1,0:T(8,128)(2,1)} async-done(((bf16[256,512]{1,0:T(8,128)(2,1)}), bf16[128,512]{1,0:T(8,128)(2,1)}) %reduce-scatter.5.cloned.1.call-update) | async-done | bytes 131088 | tf_op jit(solution)/shard_map/reduce_scatter | solution.py:82
  173.9 11.8 %all_to_all.19 = bf16[8,16,512]{2,1,0:T(8,128)(2,1)S(1)} all-to-all(bf16[8,16,512]{2,1,0:T(8,128)(2,1)} %bitcast.18), channel_id=1, replica_groups=mesh['seq'=2,'hist'=8,'chan'=2] {'hist'}, dimensions={0} | all-to-all | bytes 262144 | tf_op jit(solution)/shard_map/all_to_all | solution.py:83
  185.7 0.7 copy.8
  (12 shorter events, 0.1 us)
Async XLA Ops:
  6.5 156.0 %copy-start = (bf16[2048,512]{1,0:T(8,128)(2,1)S(1)}, bf16[2048,512]{1,0:T(8,128)(2,1)}, u32[]{:S(2)}) copy-start(bf16[2048,512]{1,0:T(8,128)(2,1)} %param.7) | copy-start | bytes 6291460
  6.5 6.1 %copy-start.1 = (bf16[256,2048]{1,0:T(8,128)(2,1)S(1)}, bf16[256,2048]{1,0:T(8,128)(2,1)}, u32[]{:S(2)}) copy-start(bf16[256,2048]{1,0:T(8,128)(2,1)} %param.4) | copy-start | bytes 3145732
  6.5 114.7 %reduce-scatter.3.cloned.1.call-start = ((), (), s32[]{:S(2)}) async-start(), calls=%async_computation.3 | async-start | bytes 2359296 | tf_op jit(solution)/shard_map/reduce_scatter | solution.py:62
  6.5 27.3 %collective-permute-start = (bf16[256,2048]{1,0:T(8,128)(2,1)}, bf16[256,2048]{1,0:T(8,128)(2,1)S(1)}, u32[]{:S(2)}, u32[]{:S(2)}) collective-permute-start(bf16[256,2048]{1,0:T(8,128)(2,1)} %param.5), channel_id=1, source_target_pairs={{2,0},{4,2},{6,4},{8,6},{10,8},{12,10},{14,12},{3,1},{5,3},{7,5},{... | collective-permute-start | bytes 3145736 | tf_op jit(solution)/shard_map/ppermute | solution.py:12
  12.6 1.3 copy-start.2
  44.9 76.4 %copy-start.3 = (bf16[32,2048]{1,0:T(8,128)(2,1)S(1)}, bf16[32,2048]{1,0:T(8,128)(2,1)}, u32[]{:S(2)}) copy-start(bf16[32,2048]{1,0:T(8,128)(2,1)} %param.6) | copy-start | bytes 393220
  52.4 110.2 %all-gather.2.cloned.1.call-start = ((), (), s32[]{:S(2)}) async-start(), calls=%async_computation.4 | async-start | bytes 1179648 | tf_op jit(solution)/shard_map/all_gather | solution.py:72
  122.9 50.9 %reduce-scatter.5.cloned.1.call-start = ((), (), s32[]{:S(2)}) async-start(), calls=%async_computation.5 | async-start | bytes 393216 | tf_op jit(solution)/shard_map/reduce_scatter | solution.py:82
Sparse Core Ops, SparseCore 0:
  52.5 68.7 reduce-scatter.2
  123.4 39.0 all-gather.1
  165.3 8.4 reduce-scatter.4
where the time goes:
time: 195 us; the launch traced here: 193 us
  waiting for transfers between devices  135 us (69%)
  matrix products  23 us (12%)
  between operations  13.2 us (7%)
  blocking collectives  11.8 us (6%)
  other arithmetic  6.15 us (3%)
    reduce_scatter x1, waiting for transfers between devices, local(): lax.psum_scatter(inverse_part(real_part, imag_part, block_tokens, period,...  68.8 us
    all_gather x1, waiting for transfers between devices, local(): lax.all_gather(gated, 'hist', axis=0, tiled=True)  39.6 us
    ppermute x1, waiting for transfers between devices, shifted(): lax.ppermute(value, axis, [(source, source + steps) for source in range(i...  18.4 us
    all_to_all x1, blocking collectives, local(): lax.all_to_all(summed, 'hist', split_axis=0, concat_axis=1, tiled=True)  11.8 us
    reduce_scatter x1, waiting for transfers between devices, local(): lax.psum_scatter(ordered.astype(jnp.bfloat16), 'chan', scatter_dimension=...  8.65 us
    dot_general x1, matrix products, inverse_part(): jnp.dot(jnp.cos(phases), real_part, precision=lax.Precision.HIGHEST, pref...  7.43 us
    dot_general x1, matrix products, inverse_part(): jnp.dot(jnp.sin(phases), imag_part, precision=lax.Precision.HIGHEST, pref...  6.21 us
    sin x1, other arithmetic, local(): table = jnp.concatenate([jnp.cos(angles), jnp.sin(angles)], 0)  4.09 us
  transfers between devices with their start and end apart: 4, of which 4 were waited for; matrix products, arithmetic and copies ran while one was open for 4% of the time, Pallas kernels for 0%

commit v1 on v0

v1 whole, which is shorter than its diff:
```python
import functools
import math

import jax
import jax.numpy as jnp
import numpy as np
from jax import lax
from jax.experimental import pallas as pl
from jax.experimental.pallas import tpu as pltpu
from jax.sharding import PartitionSpec as P

MESH = pl.DeviceIdType.MESH
BF16 = jnp.bfloat16
F32 = jnp.float32
CHUNKS = 4


def tables(local_rows, block_tokens):
    period = local_rows + block_tokens
    modes = period // 2
    odd = 2 * np.arange(modes) + 1
    turn = math.pi / period
    places = np.arange(period)
    phase = (np.outer(odd, places) % (2 * period)) * turn
    forward = np.concatenate([np.cos(phase), np.sin(phase)], 0)
    lags = block_tokens - 1 - np.arange(block_tokens)
    phase = (np.outer(lags, odd) % (2 * period)) * turn
    inverse = np.concatenate([np.cos(phase), -np.sin(phase)], 1) * (2.0 / period)
    return forward, inverse


def spectrum_product(taps, values):
    half = taps.shape[0] // 2
    tc, ts, vc, vs = taps[:half], taps[half:], values[:half], values[half:]
    return tc * vc + ts * vs, tc * vs - ts * vc


def dot(a, b):
    return jnp.dot(a, b, preferred_element_type=F32)


def local_general(history, filter_taps, gate_values, out_weight):
    local_rows, channels = history.shape
    owned_rows = gate_values.shape[0]
    count_hist = lax.axis_size("hist")
    count_chan = lax.axis_size("chan")
    block_tokens = owned_rows * count_hist
    forward, inverse = tables(local_rows, block_tokens)
    forward = jnp.asarray(forward, F32)
    forward_high = forward.astype(BF16)
    forward_low = (forward - forward_high.astype(F32)).astype(BF16)
    inverse = jnp.asarray(inverse, F32)
    next_taps = lax.ppermute(
        filter_taps, "hist", [(source, source - 1) for source in range(1, count_hist)]
    )
    extended = jnp.concatenate([filter_taps, next_taps], 0)[: forward.shape[1]]
    spec_taps = dot(forward_high, extended) + dot(forward_low, extended)
    spec_input = dot(forward_high[:, :local_rows], history) + dot(
        forward_low[:, :local_rows], history
    )
    spectrum = jnp.concatenate(spectrum_product(spec_taps, spec_input), 0)
    partial_conv = jnp.dot(
        inverse, spectrum, precision=lax.Precision.HIGHEST, preferred_element_type=F32
    )
    conv = lax.psum_scatter(partial_conv, "hist", scatter_dimension=0, tiled=True)
    gated = (conv * gate_values.astype(F32)).astype(BF16)
    partial_value = dot(lax.all_gather(gated, "hist", axis=0, tiled=True), out_weight)
    columns = partial_value.shape[1]
    half_rows = owned_rows // count_chan
    ordered = partial_value.reshape(count_hist, count_chan, half_rows, columns)
    ordered = ordered.transpose(1, 0, 2, 3).reshape(-1, columns)
    summed = lax.psum_scatter(ordered.astype(BF16), "chan", scatter_dimension=0, tiled=True)
    return lax.all_to_all(summed, "hist", split_axis=0, concat_axis=1, tiled=True)


def kernel(
    pairs, chunks, hist_ref, taps_ref, gate_ref, weight_ref, fwd_ref, inv_ref, out_ref,
    taps_buf, hist_buf, gate_buf, weight_buf, fwd_buf, inv_buf,
    send_buf, own_buf, recv_buf, gated_buf, acc_buf, swap_send, swap_recv, fin_buf, res_buf,
    load_sem, own_sem, xt_send, xt_recv, xh_send, xh_recv, xg_send, xg_recv,
    zt_send, zt_recv, rs_send, rs_recv, az_send, az_recv, ay_send, ay_recv,
    sw_send, sw_recv, fin_send, fin_recv,
):
    me = lax.axis_index("hist")
    core = lax.axis_index("chan")
    p = me // 2
    q = me % 2
    total = 2 * pairs
    rows = hist_ref.shape[0]
    half = hist_ref.shape[1] // 2
    width = half // chunks
    columns = weight_ref.shape[1]
    partner = 2 * p + (1 - q)
    modes = fwd_buf.shape[0] // 2

    def remote(src, dst, send, recv, where):
        return pltpu.make_async_remote_copy(
            src_ref=src, dst_ref=dst, send_sem=send, recv_sem=recv,
            device_id=where, device_id_type=MESH,
        )

    def cols(side, ch):
        return pl.ds(pl.multiple_of(side * half + ch * width, width), width)

    barrier = pltpu.get_barrier_semaphore()
    for d in range(1, total):
        pl.semaphore_signal(
            barrier, inc=1, device_id={"hist": (me + d) % total}, device_id_type=MESH
        )
    pl.semaphore_signal(barrier, inc=1, device_id={"chan": 1 - core}, device_id_type=MESH)

    own = []
    for ch in range(chunks):
        own.append((
            pltpu.make_async_copy(taps_ref.at[:, cols(q, ch)], taps_buf.at[q, ch], own_sem.at[0, ch]),
            pltpu.make_async_copy(hist_ref.at[:, cols(q, ch)], hist_buf.at[q, ch], own_sem.at[1, ch]),
        ))
        for copy in own[-1]:
            copy.start()
    gate_side = pl.ds(pl.multiple_of(q * half, half), half)
    gate_other = pl.ds(pl.multiple_of((1 - q) * half, half), half)
    loads = [
        pltpu.make_async_copy(fwd_ref, fwd_buf, load_sem.at[0]),
        pltpu.make_async_copy(inv_ref, inv_buf, load_sem.at[1]),
        pltpu.make_async_copy(gate_ref.at[:, gate_side], gate_buf.at[q], load_sem.at[2]),
        pltpu.make_async_copy(weight_ref, weight_buf, load_sem.at[3]),
    ]
    for copy in loads:
        copy.start()

    @pl.when(p == pairs - 1)
    def _():
        taps_buf[2] = jnp.zeros(taps_buf.shape[1:], BF16)

    pl.semaphore_wait(barrier, total)

    xt, xh, zt = [], [], []
    for ch in range(chunks):
        xt.append(remote(taps_ref.at[:, cols(1 - q, ch)], taps_buf.at[q, ch],
                         xt_send.at[ch], xt_recv.at[ch], {"hist": partner}))
        xt[-1].start()
    for ch in range(chunks):
        xh.append(remote(hist_ref.at[:, cols(1 - q, ch)], hist_buf.at[q, ch],
                         xh_send.at[ch], xh_recv.at[ch], {"hist": partner}))
        xh[-1].start()
        if ch == 0:
            xg = remote(gate_ref.at[:, gate_other], gate_buf.at[q], xg_send, xg_recv,
                        {"hist": partner})
            xg.start()
    for ch in range(chunks):
        zt.append(remote(taps_buf.at[0, ch], taps_buf.at[2, ch], zt_send.at[ch], zt_recv.at[ch],
                         {"hist": jnp.maximum(me - 2, 0)}))
    for ch in range(chunks):
        own[ch][0].wait()

        @pl.when((q == 0) & (p > 0))
        def _():
            zt[ch].start()

    for ch in range(chunks):
        xt[ch].wait_recv()

        @pl.when((q == 1) & (p > 0))
        def _():
            zt[ch].start()

    loads[0].wait()
    loads[1].wait()

    rs, az, ay = {}, {}, {}

    def compute(ch):
        own[ch][1].wait()

        @pl.when(p < pairs - 1)
        def _():
            zt[ch].wait_recv()

        t0, t1, t2 = (taps_buf[i, ch] for i in range(3))
        first = fwd_buf[:, :rows]
        second = fwd_buf[:, rows:]
        s_a = dot(first, t0) + dot(second, t1)
        s_b = dot(first, t1) + dot(second, t2)
        xh[ch].wait_recv()
        h_a = dot(first, hist_buf[0, ch])
        h_b = dot(first, hist_buf[1, ch])
        ra, ia = spectrum_product(s_a, h_a)
        rb, ib = spectrum_product(s_b, h_b)
        conv = dot(inv_buf[:, :modes], (ra + rb).astype(BF16)) + dot(
            inv_buf[:, modes:], (ia + ib).astype(BF16)
        )
        conv = conv.reshape(pairs, conv.shape[0] // pairs, width)
        send_buf[ch] = conv.astype(BF16)
        own_buf[ch] = conv
        for d in range(1, pairs):
            to = (p + d) % pairs
            rs[ch, d] = remote(send_buf.at[ch, to], recv_buf.at[ch, d - 1],
                               rs_send.at[ch, d - 1], rs_recv.at[ch, d - 1],
                               {"hist": 2 * to + q})
            rs[ch, d].start()

    def reduce(ch):
        if ch == 0:
            loads[2].wait()
            xg.wait_recv()
        value = own_buf[ch, p]
        for d in range(1, pairs):
            rs[ch, d].wait_recv()
            value = value + recv_buf[ch, d - 1].astype(F32)
        gates = gate_buf[:, :, ch * width:(ch + 1) * width].astype(F32)
        gated = (value * gates.reshape(value.shape)).astype(BF16)
        gated_buf[ch, q, p] = gated
        slot = gated_buf.at[ch, q, p]
        for d in range(1, pairs):
            az[ch, d] = remote(slot, slot, az_send.at[ch, d - 1], az_recv.at[ch, d - 1],
                               {"hist": 2 * ((p + d) % pairs) + q})
            az[ch, d].start()
        ay[ch, 0] = remote(slot, slot, ay_send.at[ch, 0], ay_recv.at[ch, 0], {"hist": partner})
        ay[ch, 0].start()

    def forward(ch):
        for d in range(1, pairs):
            az[ch, d].wait_recv()
            slot = gated_buf.at[ch, q, (p - d + pairs) % pairs]
            ay[ch, d] = remote(slot, slot, ay_send.at[ch, d], ay_recv.at[ch, d], {"hist": partner})
            ay[ch, d].start()

    def project(ch):
        if ch == 0:
            loads[3].wait()
        for d in range(pairs):
            ay[ch, d].wait_recv()
        low = gated_buf[ch, 0].reshape(-1, width)
        high = gated_buf[ch, 1].reshape(-1, width)
        value = dot(low, weight_buf[ch * width:(ch + 1) * width]) + dot(
            high, weight_buf[half + ch * width:half + (ch + 1) * width]
        )
        value = value.reshape(acc_buf.shape)
        if ch == 0:
            acc_buf[...] = value
        else:
            acc_buf[...] += value

    for step in range(chunks + 3):
        if step < chunks:
            compute(step)
        if 0 <= step - 1 < chunks:
            reduce(step - 1)
        if 0 <= step - 2 < chunks:
            forward(step - 2)
        if 0 <= step - 3 < chunks:
            project(step - 3)

    swap_send[...] = acc_buf[:, 1 - core].astype(BF16)
    swap = remote(swap_send, swap_recv, sw_send, sw_recv, {"chan": 1 - core})
    swap.start()
    swap.wait_recv()
    fin_buf[...] = (acc_buf[:, core] + swap_recv[...].astype(F32)).astype(BF16)
    fin = []
    for d in range(1, total):
        to = (me + d) % total
        fin.append(remote(fin_buf.at[to], res_buf.at[me], fin_send.at[d - 1], fin_recv.at[d - 1],
                          {"hist": to}))
        fin[-1].start()
    res_buf[me] = fin_buf[me]

    for ch in range(chunks):
        xt[ch].wait_send()
        xh[ch].wait_send()

        @pl.when(p > 0)
        def _():
            zt[ch].wait_send()

    xg.wait_send()
    for group in (rs, az, ay):
        for copy in group.values():
            copy.wait_send()
    swap.wait_send()
    for copy in fin:
        copy.wait_recv()
    for k in range(total):
        out_ref[:, k * columns:(k + 1) * columns] = res_buf[k]
    for copy in fin:
        copy.wait_send()


def local_kernel(chunks, history, filter_taps, gate_values, out_weight):
    rows, channels = history.shape
    owned = gate_values.shape[0]
    total = lax.axis_size("hist")
    cores = lax.axis_size("chan")
    pairs = total // 2
    tokens = owned * total
    half = channels // 2
    width = half // chunks
    columns = out_weight.shape[1]
    part = owned // cores
    forward, inverse = tables(rows, tokens)
    modes2 = forward.shape[0]
    forward = jnp.asarray(forward, F32).astype(BF16)
    inverse = jnp.asarray(inverse, F32).astype(BF16)
    dma = pltpu.SemaphoreType.DMA
    others = pairs - 1
    scratch = [
        pltpu.VMEM((3, chunks, rows, width), BF16),
        pltpu.VMEM((2, chunks, rows, width), BF16),
        pltpu.VMEM((2, owned, half), BF16),
        pltpu.VMEM(out_weight.shape, BF16),
        pltpu.VMEM(forward.shape, BF16),
        pltpu.VMEM(inverse.shape, BF16),
        pltpu.VMEM((chunks, pairs, 2 * owned, width), BF16),
        pltpu.VMEM((chunks, pairs, 2 * owned, width), F32),
        pltpu.VMEM((chunks, others, 2 * owned, width), BF16),
        pltpu.VMEM((chunks, 2, pairs, 2 * owned, width), BF16),
        pltpu.VMEM((total, cores, part, columns), F32),
        pltpu.VMEM((total, part, columns), BF16),
        pltpu.VMEM((total, part, columns), BF16),
        pltpu.VMEM((total, part, columns), BF16),
        pltpu.VMEM((total, part, columns), BF16),
        dma((4,)), dma((2, chunks)),
        dma((chunks,)), dma((chunks,)), dma((chunks,)), dma((chunks,)), dma, dma,
        dma((chunks,)), dma((chunks,)),
        dma((chunks, others)), dma((chunks, others)),
        dma((chunks, others)), dma((chunks, others)),
        dma((chunks, pairs)), dma((chunks, pairs)),
        dma, dma, dma((total - 1,)), dma((total - 1,)),
    ]
    return pl.pallas_call(
        functools.partial(kernel, pairs, chunks),
        out_shape=jax.ShapeDtypeStruct((part, total * columns), BF16),
        in_specs=[pl.BlockSpec(memory_space=pl.ANY)] * 6,
        out_specs=pl.BlockSpec(memory_space=pltpu.VMEM),
        scratch_shapes=scratch,
        compiler_params=pltpu.CompilerParams(
            collective_id=0, has_side_effects=True, vmem_limit_bytes=32 * 1024 * 1024
        ),
    )(history, filter_taps, gate_values, out_weight, forward, inverse)


def local(history, filter_taps, gate_values, out_weight):
    rows, channels = history.shape
    owned = gate_values.shape[0]
    total = lax.axis_size("hist")
    cores = lax.axis_size("chan")
    fits = (
        total % 2 == 0
        and total >= 4
        and cores == 2
        and owned % (16 * cores) == 0
        and rows == owned * total
        and channels % (256 * CHUNKS) == 0
        and out_weight.shape[1] % 128 == 0
    )
    if fits:
        return local_kernel(CHUNKS, history, filter_taps, gate_values, out_weight)
    return local_general(history, filter_taps, gate_values, out_weight)


def solution(mesh):
    return jax.shard_map(
        local,
        mesh=mesh,
        in_specs=(
            P(("seq", "hist"), "chan"),
            P("hist", "chan"),
            P(("seq", "hist"), "chan"),
            P("chan", "hist"),
        ),
        out_specs=P(("seq", "hist", "chan"), None),
        check_vma=False,
    )
```

time: 195 us -> 65.3 us (0.33)
  waiting for transfers between devices: 135 us -> 0 us
  Pallas kernels: 0 us -> 57.2 us
  matrix products: 23 us -> 0 us
  between operations: 13.2 us -> 0.02 us
  blocking collectives: 11.8 us -> 0 us
  other arithmetic: 6.15 us -> 0 us
  local copies, waits for them, and re-layouts: 1.6 us -> 7.59 us
    reduce_scatter x2 -> x0, waiting for transfers between devices: 77.5 us -> none  [the longest x1 68.8 us: local(): lax.psum_scatter(inverse_part(real_part, imag_part, block_tokens, period,...]
    pallas_call x0 -> x1, Pallas kernels: none -> 57.2 us  [local_kernel(): pl.pallas_call(functools.partial(kernel, pairs, chunks), out_shape=jax.Sh...]
    all_gather x1 -> x0, waiting for transfers between devices: 39.6 us -> none  [local(): lax.all_gather(gated, 'hist', axis=0, tiled=True)]
    dot_general x7 -> x0, matrix products: 23 us -> none  [the longest x1 7.43 us: inverse_part(): jnp.dot(jnp.cos(phases), real_part, precision=lax.Precision.HIGHEST, pref...]
    ppermute x1 -> x0, waiting for transfers between devices: 18.4 us -> none  [shifted(): lax.ppermute(value, axis, [(source, source + steps) for source in range(i...]
    all_to_all x1 -> x0, blocking collectives: 11.8 us -> none  [local(): lax.all_to_all(summed, 'hist', split_axis=0, concat_axis=1, tiled=True)]
    unnamed x9 -> x13, local copies, waits for them, and re-layouts: 0.12 us -> 7.59 us
    sin x1 -> x0, other arithmetic: 4.09 us -> none  [local(): table = jnp.concatenate([jnp.cos(angles), jnp.sin(angles)], 0)]
  transfers between devices with their start and end apart: 4 -> 0, of which waited for: 4 -> 0; matrix products, arithmetic and copies ran while one was open for 4% -> 0% of each run, Pallas kernels for 0% -> 0%
where the time goes in v1:
time: 65.3 us; the launch traced here: 64.9 us
  Pallas kernels  57.2 us (88%)
  local copies, waits for them, and re-layouts  7.59 us (12%)
    pallas_call x1, Pallas kernels, local_kernel(): pl.pallas_call(functools.partial(kernel, pairs, chunks), out_shape=jax.Sh...  57.2 us
    unnamed x13, local copies, waits for them, and re-layouts  7.59 us

profile of v1, /device:TPU:1, one launch (start us, length us, event | category | flops | bytes accessed | tf_op | source)
XLA Modules:
  0.0 64.9 jit_solution(2009844426435098071)
XLA Ops:
  0.0 0.0 copy-start
  0.0 1.6 %copy-done = bf16[2048,512]{1,0:T(8,128)(2,1)S(1)} copy-done((bf16[2048,512]{1,0:T(8,128)(2,1)S(1)}, bf16[2048,512]{1,0:T(8,128)(2,1)}, u32[]{:S(2)}) %copy-start) | copy-done | bytes 2097176
  1.6 0.0 copy-start.1
  1.6 1.2 %copy-done.1 = bf16[256,2048]{1,0:T(8,128)(2,1)S(1)} copy-done((bf16[256,2048]{1,0:T(8,128)(2,1)S(1)}, bf16[256,2048]{1,0:T(8,128)(2,1)}, u32[]{:S(2)}) %copy-start.1) | copy-done | bytes 1048600
  2.8 0.0 copy-start.2
  2.8 1.2 %copy-done.2 = bf16[256,2048]{1,0:T(8,128)(2,1)S(1)} copy-done((bf16[256,2048]{1,0:T(8,128)(2,1)S(1)}, bf16[256,2048]{1,0:T(8,128)(2,1)}, u32[]{:S(2)}) %copy-start.2) | copy-done | bytes 1048600
  4.0 0.0 copy-start.3
  4.0 1.0 %copy-done.3 = bf16[512,512]{1,0:T(8,128)(2,1)S(1)} copy-done((bf16[512,512]{1,0:T(8,128)(2,1)S(1)}, bf16[512,512]{1,0:T(8,128)(2,1)}, u32[]{:S(2)}) %copy-start.3) | copy-done | bytes 524312
  5.1 0.0 copy-start.4
  5.1 0.9 %copy-done.4 = bf16[256,512]{1,0:T(8,128)(2,1)S(1)} copy-done((bf16[256,512]{1,0:T(8,128)(2,1)S(1)}, bf16[256,512]{1,0:T(8,128)(2,1)}, u32[]{:S(2)}) %copy-start.4) | copy-done | bytes 262168
  6.0 0.0 copy-start.5
  6.0 0.9 %copy-done.5 = bf16[32,2048]{1,0:T(8,128)(2,1)S(1)} copy-done((bf16[32,2048]{1,0:T(8,128)(2,1)S(1)}, bf16[32,2048]{1,0:T(8,128)(2,1)}, u32[]{:S(2)}) %copy-start.5) | copy-done | bytes 131096
  6.9 57.2 %shard_map.64 = bf16[16,4096]{1,0:T(8,128)(2,1)S(1)} custom-call(bf16[256,2048]{1,0:T(8,128)(2,1)S(1)} %copy-done.1, bf16[256,2048]{1,0:T(8,128)(2,1)S(1)} %copy-done.2, bf16[32,2048]{1,0:T(8,128)(2,1)S(1)} %copy-done.5, bf16[2048,512]{1,0:T(8,128)(2,1)S(1)} %copy-done, bf16[512,512]{1,0:T(8,128)(2,1)S(1)} %copy-done.3, bf16[256,512]{1,0:T(8,128)(2,1)S(1)} %copy-done.4), custom_call_target="tpu_custom_call" | custom-call | tf_op jit(solution)/shard_map/pallas_call | solution.py:329
  64.2 0.7 %copy.8 = bf16[16,4096]{1,0:T(8,128)(2,1)} copy(bf16[16,4096]{1,0:T(8,128)(2,1)S(1)} %shard_map.64) | data formatting | bytes 262144
Async XLA Ops:
  0.0 1.6 %copy-start = (bf16[2048,512]{1,0:T(8,128)(2,1)S(1)}, bf16[2048,512]{1,0:T(8,128)(2,1)}, u32[]{:S(2)}) copy-start(bf16[2048,512]{1,0:T(8,128)(2,1)} %weight_ref.1) | copy-start | bytes 6291460
  1.6 1.2 %copy-start.1 = (bf16[256,2048]{1,0:T(8,128)(2,1)S(1)}, bf16[256,2048]{1,0:T(8,128)(2,1)}, u32[]{:S(2)}) copy-start(bf16[256,2048]{1,0:T(8,128)(2,1)} %hist_ref.1) | copy-start | bytes 3145732
  2.8 1.2 %copy-start.2 = (bf16[256,2048]{1,0:T(8,128)(2,1)S(1)}, bf16[256,2048]{1,0:T(8,128)(2,1)}, u32[]{:S(2)}) copy-start(bf16[256,2048]{1,0:T(8,128)(2,1)} %taps_ref.1) | copy-start | bytes 3145732
  4.0 1.0 %copy-start.3 = (bf16[512,512]{1,0:T(8,128)(2,1)S(1)}, bf16[512,512]{1,0:T(8,128)(2,1)}, u32[]{:S(2)}) copy-start(bf16[512,512]{1,0:T(8,128)(2,1)} %constant.6.fwd_ref) | copy-start | bytes 1572868
  5.1 0.9 %copy-start.4 = (bf16[256,512]{1,0:T(8,128)(2,1)S(1)}, bf16[256,512]{1,0:T(8,128)(2,1)}, u32[]{:S(2)}) copy-start(bf16[256,512]{1,0:T(8,128)(2,1)} %constant.7.inv_ref) | copy-start | bytes 786436
  6.0 0.9 %copy-start.5 = (bf16[32,2048]{1,0:T(8,128)(2,1)S(1)}, bf16[32,2048]{1,0:T(8,128)(2,1)}, u32[]{:S(2)}) copy-start(bf16[32,2048]{1,0:T(8,128)(2,1)} %gate_ref.1) | copy-start | bytes 393220

commit v2 on v1

--- a/solution.py
+++ b/solution.py
@@ -78,11 +78,12 @@
     taps_buf, hist_buf, gate_buf, weight_buf, fwd_buf, inv_buf,
     send_buf, own_buf, recv_buf, gated_buf, acc_buf, swap_send, swap_recv, fin_buf, res_buf,
     load_sem, own_sem, xt_send, xt_recv, xh_send, xh_recv, xg_send, xg_recv,
-    zt_send, zt_recv, rs_send, rs_recv, az_send, az_recv, ay_send, ay_recv,
+    zt_send, zt_recv, xf_send, xf_recv, xz_send, xz_recv, rs_send, rs_recv, az_send, az_recv, ay_send, ay_recv,
     sw_send, sw_recv, fin_send, fin_recv,
 ):
     me = lax.axis_index("hist")
     core = lax.axis_index("chan")
+    seq = lax.axis_index("seq")
     p = me // 2
     q = me % 2
     total = 2 * pairs
@@ -108,6 +109,7 @@
             barrier, inc=1, device_id={"hist": (me + d) % total}, device_id_type=MESH
         )
     pl.semaphore_signal(barrier, inc=1, device_id={"chan": 1 - core}, device_id_type=MESH)
+    pl.semaphore_signal(barrier, inc=1, device_id={"seq": 1 - seq}, device_id_type=MESH)
 
     own = []
     for ch in range(chunks):
@@ -132,13 +134,27 @@
     def _():
         taps_buf[2] = jnp.zeros(taps_buf.shape[1:], BF16)
 
-    pl.semaphore_wait(barrier, total)
-
-    xt, xh, zt = [], [], []
-    for ch in range(chunks):
-        xt.append(remote(taps_ref.at[:, cols(1 - q, ch)], taps_buf.at[q, ch],
-                         xt_send.at[ch], xt_recv.at[ch], {"hist": partner}))
+    pl.semaphore_wait(barrier, total + 1)
+
+    xt, xh, zt, xf, xz = [], [], [], [], []
+    for j in range(chunks // 2):
+        mine = 2 * j + seq
+        xt.append(remote(taps_ref.at[:, cols(1 - q, mine)], taps_buf.at[q, mine],
+                         xt_send.at[j], xt_recv.at[j], {"hist": partner}))
         xt[-1].start()
+        before = {"hist": jnp.maximum(me - 2, 0)}
+        zt.append(remote(taps_buf.at[0, mine], taps_buf.at[2, mine],
+                         zt_send.at[j], zt_recv.at[j], before))
+        xf.append(remote(taps_buf.at[1 - q, mine], taps_buf.at[1 - q, mine],
+                         xf_send.at[j], xf_recv.at[j], {"seq": 1 - seq}))
+        xz.append(remote(taps_buf.at[2, mine], taps_buf.at[2, mine],
+                         xz_send.at[j], xz_recv.at[j], {"seq": 1 - seq}))
+
+        @pl.when((q == 0) & (p > 0))
+        def _():
+            remote(taps_ref.at[:, cols(0, mine)], taps_buf.at[2, mine],
+                   zt_send.at[j], zt_recv.at[j], before).start()
+
     for ch in range(chunks):
         xh.append(remote(hist_ref.at[:, cols(1 - q, ch)], hist_buf.at[q, ch],
                          xh_send.at[ch], xh_recv.at[ch], {"hist": partner}))
@@ -147,22 +163,19 @@
             xg = remote(gate_ref.at[:, gate_other], gate_buf.at[q], xg_send, xg_recv,
                         {"hist": partner})
             xg.start()
-    for ch in range(chunks):
-        zt.append(remote(taps_buf.at[0, ch], taps_buf.at[2, ch], zt_send.at[ch], zt_recv.at[ch],
-                         {"hist": jnp.maximum(me - 2, 0)}))
-    for ch in range(chunks):
-        own[ch][0].wait()
-
-        @pl.when((q == 0) & (p > 0))
-        def _():
-            zt[ch].start()
-
-    for ch in range(chunks):
-        xt[ch].wait_recv()
+    for j in range(chunks // 2):
+        xt[j].wait_recv()
+        xf[j].start()
 
         @pl.when((q == 1) & (p > 0))
         def _():
-            zt[ch].start()
+            zt[j].start()
+
+    for j in range(chunks // 2):
+        @pl.when(p < pairs - 1)
+        def _():
+            zt[j].wait_recv()
+            xz[j].start()
 
     loads[0].wait()
     loads[1].wait()
@@ -170,11 +183,14 @@
     rs, az, ay = {}, {}, {}
 
     def compute(ch):
-        own[ch][1].wait()
-
-        @pl.when(p < pairs - 1)
-        def _():
-            zt[ch].wait_recv()
+        for copy in own[ch]:
+            copy.wait()
+        if ch % 2 == 0:
+            xf[ch // 2].wait_recv()
+
+            @pl.when(p < pairs - 1)
+            def _():
+                xz[ch // 2].wait_recv()
 
         t0, t1, t2 = (taps_buf[i, ch] for i in range(3))
         first = fwd_buf[:, :rows]
@@ -265,12 +281,18 @@
     res_buf[me] = fin_buf[me]
 
     for ch in range(chunks):
-        xt[ch].wait_send()
         xh[ch].wait_send()
+    for j in range(chunks // 2):
+        xt[j].wait_send()
+        xf[j].wait_send()
 
         @pl.when(p > 0)
         def _():
-            zt[ch].wait_send()
+            zt[j].wait_send()
+
+        @pl.when(p < pairs - 1)
+        def _():
+            xz[j].wait_send()
 
     xg.wait_send()
     for group in (rs, az, ay):
@@ -319,8 +341,9 @@
         pltpu.VMEM((total, part, columns), BF16),
         pltpu.VMEM((total, part, columns), BF16),
         dma((4,)), dma((2, chunks)),
-        dma((chunks,)), dma((chunks,)), dma((chunks,)), dma((chunks,)), dma, dma,
-        dma((chunks,)), dma((chunks,)),
+        dma((chunks // 2,)), dma((chunks // 2,)), dma((chunks,)), dma((chunks,)), dma, dma,
+        dma((chunks // 2,)), dma((chunks // 2,)), dma((chunks // 2,)), dma((chunks // 2,)),
+        dma((chunks // 2,)), dma((chunks // 2,)),
         dma((chunks, others)), dma((chunks, others)),
         dma((chunks, others)), dma((chunks, others)),
         dma((chunks, pairs)), dma((chunks, pairs)),
@@ -333,7 +356,7 @@
         out_specs=pl.BlockSpec(memory_space=pltpu.VMEM),
         scratch_shapes=scratch,
         compiler_params=pltpu.CompilerParams(
-            collective_id=0, has_side_effects=True, vmem_limit_bytes=32 * 1024 * 1024
+            collective_id=0, has_side_effects=True, vmem_limit_bytes=67043328
         ),
     )(history, filter_taps, gate_values, out_weight, forward, inverse)
 
@@ -347,6 +370,8 @@
         total % 2 == 0
         and total >= 4
         and cores == 2
+        and lax.axis_size("seq") == 2
+        and CHUNKS % 2 == 0
         and owned % (16 * cores) == 0
         and rows == owned * total
         and channels % (256 * CHUNKS) == 0

time: 65.3 us -> 59.4 us (0.910)
  local copies, waits for them, and re-layouts: 7.59 us -> 1.57 us
    unnamed x13 -> x1, local copies, waits for them, and re-layouts: 7.59 us -> 1.57 us
where the time goes in v2:
time: 59.4 us; the launch traced here: 59.3 us
  Pallas kernels  57.7 us (97%)
  local copies, waits for them, and re-layouts  1.57 us (3%)
    pallas_call x1, Pallas kernels, local_kernel(): pl.pallas_call(functools.partial(kernel, pairs, chunks), out_shape=jax.Sh...  57.7 us
    unnamed x1, local copies, waits for them, and re-layouts  1.57 us

profile of v2, /device:TPU:1, one launch (start us, length us, event | category | flops | bytes accessed | tf_op | source)
XLA Modules:
  0.0 59.3 jit_solution(10649356615897543713)
XLA Ops:
  0.0 57.7 %shard_map.64 = bf16[16,4096]{1,0:T(8,128)(2,1)} custom-call(bf16[256,2048]{1,0:T(8,128)(2,1)} %hist_ref.1, bf16[256,2048]{1,0:T(8,128)(2,1)} %taps_ref.1, bf16[32,2048]{1,0:T(8,128)(2,1)} %gate_ref.1, bf16[2048,512]{1,0:T(8,128)(2,1)} %weight_ref.1, bf16[512,512]{1,0:T(8,128)(2,1)} %constant.6.fwd_ref, bf16[256,512]{1,0:T(8,128)(2,1)} %constant.7.inv_ref), custom_call_target="tpu_custom_call" | custom-call | tf_op jit(solution)/shard_map/pallas_call | solution.py:352
  57.7 1.6 %copy.8 = bf16[16,4096]{1,0:T(8,128)(2,1)} copy(bf16[16,4096]{1,0:T(8,128)(2,1)} %shard_map.64) | data formatting | bytes 262144

commit v3 on v2

--- a/solution.py
+++ b/solution.py
@@ -13,6 +13,9 @@
 BF16 = jnp.bfloat16
 F32 = jnp.float32
 CHUNKS = 4
+WINDOW = 3
+REDUCE_AT = 1.1
+LINE_STEP = 1.01
 
 
 def tables(local_rows, block_tokens):
@@ -78,8 +81,8 @@
     taps_buf, hist_buf, gate_buf, weight_buf, fwd_buf, inv_buf,
     send_buf, own_buf, recv_buf, gated_buf, acc_buf, swap_send, swap_recv, fin_buf, res_buf,
     load_sem, own_sem, xt_send, xt_recv, xh_send, xh_recv, xg_send, xg_recv,
-    zt_send, zt_recv, xf_send, xf_recv, xz_send, xz_recv, rs_send, rs_recv, az_send, az_recv, ay_send, ay_recv,
-    sw_send, sw_recv, fin_send, fin_recv,
+    zt_send, zt_recv, xf_send, xf_recv, rs_send, rs_recv, az_send, az_recv, ay_send, ay_recv,
+    sw_send, sw_recv, fin_send, fin_recv, ready_sem,
 ):
     me = lax.axis_index("hist")
     core = lax.axis_index("chan")
@@ -104,10 +107,18 @@
         return pl.ds(pl.multiple_of(side * half + ch * width, width), width)
 
     barrier = pltpu.get_barrier_semaphore()
-    for d in range(1, total):
-        pl.semaphore_signal(
-            barrier, inc=1, device_id={"hist": (me + d) % total}, device_id_type=MESH
-        )
+    def greet_line(sem):
+        @pl.when(p > 0)
+        def _():
+            pl.semaphore_signal(sem, inc=1, device_id={"hist": me - 2}, device_id_type=MESH)
+
+        @pl.when(p < pairs - 1)
+        def _():
+            pl.semaphore_signal(sem, inc=1, device_id={"hist": me + 2}, device_id_type=MESH)
+
+    beside = jnp.minimum(p, 1) + jnp.minimum(pairs - 1 - p, 1)
+    greet_line(barrier)
+    pl.semaphore_signal(barrier, inc=1, device_id={"hist": partner}, device_id_type=MESH)
     pl.semaphore_signal(barrier, inc=1, device_id={"chan": 1 - core}, device_id_type=MESH)
     pl.semaphore_signal(barrier, inc=1, device_id={"seq": 1 - seq}, device_id_type=MESH)
 
@@ -130,57 +141,66 @@
     for copy in loads:
         copy.start()
 
-    @pl.when(p == pairs - 1)
+    @pl.when((q == 0) & (p == pairs - 1))
     def _():
         taps_buf[2] = jnp.zeros(taps_buf.shape[1:], BF16)
 
-    pl.semaphore_wait(barrier, total + 1)
-
-    xt, xh, zt, xf, xz = [], [], [], [], []
+    @pl.when((q == 1) & (p == 0))
+    def _():
+        hist_buf[2] = jnp.zeros(hist_buf.shape[1:], BF16)
+
+    pl.semaphore_wait(barrier, 3 + beside)
+
+    xt, xh, zt, xf = [], [], [], []
     for j in range(chunks // 2):
         mine = 2 * j + seq
         xt.append(remote(taps_ref.at[:, cols(1 - q, mine)], taps_buf.at[q, mine],
                          xt_send.at[j], xt_recv.at[j], {"hist": partner}))
-        xt[-1].start()
-        before = {"hist": jnp.maximum(me - 2, 0)}
-        zt.append(remote(taps_buf.at[0, mine], taps_buf.at[2, mine],
-                         zt_send.at[j], zt_recv.at[j], before))
         xf.append(remote(taps_buf.at[1 - q, mine], taps_buf.at[1 - q, mine],
                          xf_send.at[j], xf_recv.at[j], {"seq": 1 - seq}))
-        xz.append(remote(taps_buf.at[2, mine], taps_buf.at[2, mine],
-                         xz_send.at[j], xz_recv.at[j], {"seq": 1 - seq}))
+
+    for ch in range(chunks):
+        low = remote(taps_ref.at[:, cols(0, ch)], taps_buf.at[2, ch], zt_send.at[ch],
+                     zt_recv.at[ch], {"hist": jnp.maximum(me - 2, 0)})
+        high = remote(hist_ref.at[:, cols(1, ch)], hist_buf.at[2, ch], zt_send.at[ch],
+                      zt_recv.at[ch], {"hist": jnp.minimum(me + 2, total - 1)})
+        zt.append((low, high))
 
         @pl.when((q == 0) & (p > 0))
         def _():
-            remote(taps_ref.at[:, cols(0, mine)], taps_buf.at[2, mine],
-                   zt_send.at[j], zt_recv.at[j], before).start()
+            low.start()
+
+        @pl.when((q == 1) & (p < pairs - 1))
+        def _():
+            high.start()
 
     for ch in range(chunks):
         xh.append(remote(hist_ref.at[:, cols(1 - q, ch)], hist_buf.at[q, ch],
                          xh_send.at[ch], xh_recv.at[ch], {"hist": partner}))
-        xh[-1].start()
-        if ch == 0:
-            xg = remote(gate_ref.at[:, gate_other], gate_buf.at[q], xg_send, xg_recv,
-                        {"hist": partner})
-            xg.start()
+    xg = remote(gate_ref.at[:, gate_other], gate_buf.at[q], xg_send, xg_recv, {"hist": partner})
+    queue = [(copy,) for copy in xt] + [(copy,) for copy in xh]
+    queue[len(xt) + 1] += (xg,)
+
+    def advance(i):
+        if i < len(queue):
+            for copy in queue[i]:
+                copy.start()
+
+    for i in range(WINDOW):
+        advance(i)
+    for r in range(pairs - 2):
+        greet_line(ready_sem.at[r])
+        pl.semaphore_wait(ready_sem.at[r], beside)
+
     for j in range(chunks // 2):
         xt[j].wait_recv()
+        advance(j + WINDOW)
         xf[j].start()
-
-        @pl.when((q == 1) & (p > 0))
-        def _():
-            zt[j].start()
-
-    for j in range(chunks // 2):
-        @pl.when(p < pairs - 1)
-        def _():
-            zt[j].wait_recv()
-            xz[j].start()
 
     loads[0].wait()
     loads[1].wait()
 
-    rs, az, ay = {}, {}, {}
+    rs, up, down, ay = {}, {}, {}, {}
 
     def compute(ch):
         for copy in own[ch]:
@@ -188,22 +208,31 @@
         if ch % 2 == 0:
             xf[ch // 2].wait_recv()
 
-            @pl.when(p < pairs - 1)
-            def _():
-                xz[ch // 2].wait_recv()
-
-        t0, t1, t2 = (taps_buf[i, ch] for i in range(3))
+
+        @pl.when((q == 0) & (p < pairs - 1))
+        def _():
+            zt[ch][0].wait_recv()
+
+        @pl.when((q == 1) & (p > 0))
+        def _():
+            zt[ch][1].wait_recv()
+
+        t0, t1 = taps_buf[0, ch], taps_buf[1, ch]
         first = fwd_buf[:, :rows]
         second = fwd_buf[:, rows:]
         s_a = dot(first, t0) + dot(second, t1)
-        s_b = dot(first, t1) + dot(second, t2)
+        s_b = dot(first, t1)
+        s_c = dot(second, taps_buf[2 - 2 * q, ch])
         xh[ch].wait_recv()
+        advance(len(xt) + ch + WINDOW)
         h_a = dot(first, hist_buf[0, ch])
         h_b = dot(first, hist_buf[1, ch])
+        h_c = dot(first, hist_buf[1 + q, ch])
         ra, ia = spectrum_product(s_a, h_a)
         rb, ib = spectrum_product(s_b, h_b)
-        conv = dot(inv_buf[:, :modes], (ra + rb).astype(BF16)) + dot(
-            inv_buf[:, modes:], (ia + ib).astype(BF16)
+        rc, ic = spectrum_product(s_c, h_c)
+        conv = dot(inv_buf[:, :modes], (ra + rb + rc).astype(BF16)) + dot(
+            inv_buf[:, modes:], (ia + ib + ic).astype(BF16)
         )
         conv = conv.reshape(pairs, conv.shape[0] // pairs, width)
         send_buf[ch] = conv.astype(BF16)
@@ -226,26 +255,58 @@
         gates = gate_buf[:, :, ch * width:(ch + 1) * width].astype(F32)
         gated = (value * gates.reshape(value.shape)).astype(BF16)
         gated_buf[ch, q, p] = gated
-        slot = gated_buf.at[ch, q, p]
-        for d in range(1, pairs):
-            az[ch, d] = remote(slot, slot, az_send.at[ch, d - 1], az_recv.at[ch, d - 1],
-                               {"hist": 2 * ((p + d) % pairs) + q})
-            az[ch, d].start()
-        ay[ch, 0] = remote(slot, slot, ay_send.at[ch, 0], ay_recv.at[ch, 0], {"hist": partner})
-        ay[ch, 0].start()
-
-    def forward(ch):
-        for d in range(1, pairs):
-            az[ch, d].wait_recv()
-            slot = gated_buf.at[ch, q, (p - d + pairs) % pairs]
-            ay[ch, d] = remote(slot, slot, ay_send.at[ch, d], ay_recv.at[ch, d], {"hist": partner})
-            ay[ch, d].start()
+        line(ch, 0)
+
+    def line(ch, s):
+        if s > 0:
+            left_slot = gated_buf.at[ch, q, (p - s + pairs) % pairs]
+            right_slot = gated_buf.at[ch, q, (p + s) % pairs]
+        else:
+            left_slot = right_slot = gated_buf.at[ch, q, p]
+        below = {"hist": jnp.maximum(me - 2, 0)}
+        above = {"hist": jnp.minimum(me + 2, total - 1)}
+        across = {"hist": partner}
+        up[ch, s] = remote(left_slot, left_slot, az_send.at[ch, 0, s], az_recv.at[ch, 0, s], above)
+        down[ch, s] = remote(right_slot, right_slot, az_send.at[ch, 1, s], az_recv.at[ch, 1, s], below)
+        ay[ch, 0, s] = remote(left_slot, left_slot, ay_send.at[ch, 0, s], ay_recv.at[ch, 0, s], across)
+        ay[ch, 1, s] = remote(right_slot, right_slot, ay_send.at[ch, 1, s], ay_recv.at[ch, 1, s], across)
+
+        @pl.when(p - s >= 0)
+        def _():
+            if s > 0:
+                up[ch, s - 1].wait_recv()
+
+            @pl.when(p < pairs - 1)
+            def _():
+                up[ch, s].start()
+
+            ay[ch, 0, s].start()
+
+        @pl.when(p + s < pairs)
+        def _():
+            if s > 0:
+                down[ch, s - 1].wait_recv()
+
+            @pl.when(p > 0)
+            def _():
+                down[ch, s].start()
+
+            if s > 0:
+                ay[ch, 1, s].start()
 
     def project(ch):
         if ch == 0:
             loads[3].wait()
-        for d in range(pairs):
-            ay[ch, d].wait_recv()
+        ay[ch, 0, 0].wait_recv()
+        for s in range(1, pairs):
+            @pl.when(p - s >= 0)
+            def _():
+                ay[ch, 0, s].wait_recv()
+
+            @pl.when(p + s < pairs)
+            def _():
+                ay[ch, 1, s].wait_recv()
+
         low = gated_buf[ch, 0].reshape(-1, width)
         high = gated_buf[ch, 1].reshape(-1, width)
         value = dot(low, weight_buf[ch * width:(ch + 1) * width]) + dot(
@@ -257,15 +318,15 @@
         else:
             acc_buf[...] += value
 
-    for step in range(chunks + 3):
-        if step < chunks:
-            compute(step)
-        if 0 <= step - 1 < chunks:
-            reduce(step - 1)
-        if 0 <= step - 2 < chunks:
-            forward(step - 2)
-        if 0 <= step - 3 < chunks:
-            project(step - 3)
+    events = []
+    for ch in range(chunks):
+        events.append((ch, 0, functools.partial(compute, ch)))
+        events.append((ch + REDUCE_AT, 1, functools.partial(reduce, ch)))
+        for s in range(1, pairs):
+            events.append((ch + REDUCE_AT + s * LINE_STEP, 1 + s, functools.partial(line, ch, s)))
+        events.append((ch + REDUCE_AT + pairs * LINE_STEP, 1 + pairs, functools.partial(project, ch)))
+    for event in sorted(events, key=lambda entry: entry[:2]):
+        event[2]()
 
     swap_send[...] = acc_buf[:, 1 - core].astype(BF16)
     swap = remote(swap_send, swap_recv, sw_send, sw_recv, {"chan": 1 - core})
@@ -285,19 +346,39 @@
     for j in range(chunks // 2):
         xt[j].wait_send()
         xf[j].wait_send()
-
-        @pl.when(p > 0)
-        def _():
-            zt[j].wait_send()
-
-        @pl.when(p < pairs - 1)
-        def _():
-            xz[j].wait_send()
+    for ch in range(chunks):
+        @pl.when((q == 0) & (p > 0))
+        def _():
+            zt[ch][0].wait_send()
+
+        @pl.when((q == 1) & (p < pairs - 1))
+        def _():
+            zt[ch][1].wait_send()
 
     xg.wait_send()
-    for group in (rs, az, ay):
-        for copy in group.values():
-            copy.wait_send()
+    for copy in rs.values():
+        copy.wait_send()
+    for ch in range(chunks):
+        ay[ch, 0, 0].wait_send()
+        for s in range(pairs):
+            @pl.when(p - s >= 0)
+            def _():
+                if s > 0:
+                    ay[ch, 0, s].wait_send()
+
+                @pl.when(p < pairs - 1)
+                def _():
+                    up[ch, s].wait_send()
+
+            @pl.when(p + s < pairs)
+            def _():
+                if s > 0:
+                    ay[ch, 1, s].wait_send()
+
+                @pl.when(p > 0)
+                def _():
+                    down[ch, s].wait_send()
+
     swap.wait_send()
     for copy in fin:
         copy.wait_recv()
@@ -326,7 +407,7 @@
     others = pairs - 1
     scratch = [
         pltpu.VMEM((3, chunks, rows, width), BF16),
-        pltpu.VMEM((2, chunks, rows, width), BF16),
+        pltpu.VMEM((3, chunks, rows, width), BF16),
         pltpu.VMEM((2, owned, half), BF16),
         pltpu.VMEM(out_weight.shape, BF16),
         pltpu.VMEM(forward.shape, BF16),
@@ -342,12 +423,12 @@
         pltpu.VMEM((total, part, columns), BF16),
         dma((4,)), dma((2, chunks)),
         dma((chunks // 2,)), dma((chunks // 2,)), dma((chunks,)), dma((chunks,)), dma, dma,
-        dma((chunks // 2,)), dma((chunks // 2,)), dma((chunks // 2,)), dma((chunks // 2,)),
-        dma((chunks // 2,)), dma((chunks // 2,)),
+        dma((chunks,)), dma((chunks,)), dma((chunks // 2,)), dma((chunks // 2,)),
         dma((chunks, others)), dma((chunks, others)),
-        dma((chunks, others)), dma((chunks, others)),
-        dma((chunks, pairs)), dma((chunks, pairs)),
+        dma((chunks, 2, pairs)), dma((chunks, 2, pairs)),
+        dma((chunks, 2, pairs)), dma((chunks, 2, pairs)),
         dma, dma, dma((total - 1,)), dma((total - 1,)),
+        pltpu.SemaphoreType.REGULAR((pairs - 2,)),
     ]
     return pl.pallas_call(
         functools.partial(kernel, pairs, chunks),
@@ -368,13 +449,13 @@
     cores = lax.axis_size("chan")
     fits = (
         total % 2 == 0
-        and total >= 4
+        and total >= 6
         and cores == 2
         and lax.axis_size("seq") == 2
         and CHUNKS % 2 == 0
         and owned % (16 * cores) == 0
         and rows == owned * total
-        and channels % (256 * CHUNKS) == 0
+        and channels % (128 * CHUNKS) == 0
         and out_weight.shape[1] % 128 == 0
     )
     if fits:

time: 59.4 us -> 52.7 us (0.89)
  Pallas kernels: 57.7 us -> 51 us
    pallas_call x1, Pallas kernels: 57.7 us -> 51 us  [local_kernel(): pl.pallas_call(functools.partial(kernel, pairs, chunks), out_shape=jax.Sh...]
where the time goes in v3:
time: 52.7 us; the launch traced here: 52.6 us
  Pallas kernels  51 us (97%)
  local copies, waits for them, and re-layouts  1.57 us (3%)
    pallas_call x1, Pallas kernels, local_kernel(): pl.pallas_call(functools.partial(kernel, pairs, chunks), out_shape=jax.Sh...  51 us
    unnamed x1, local copies, waits for them, and re-layouts  1.57 us

profile of v3, /device:TPU:1, one launch (start us, length us, event | category | flops | bytes accessed | tf_op | source)
XLA Modules:
  0.0 52.6 jit_solution(11156924250538875052)
XLA Ops:
  0.0 51.0 %shard_map.64 = bf16[16,4096]{1,0:T(8,128)(2,1)} custom-call(bf16[256,2048]{1,0:T(8,128)(2,1)} %hist_ref.1, bf16[256,2048]{1,0:T(8,128)(2,1)} %taps_ref.1, bf16[32,2048]{1,0:T(8,128)(2,1)} %gate_ref.1, bf16[2048,512]{1,0:T(8,128)(2,1)} %weight_ref.1, bf16[512,512]{1,0:T(8,128)(2,1)} %constant.6.fwd_ref, bf16[256,512]{1,0:T(8,128)(2,1)} %constant.7.inv_ref), custom_call_target="tpu_custom_call" | custom-call | tf_op jit(solution)/shard_map/pallas_call | solution.py:433
  51.0 1.6 %copy.8 = bf16[16,4096]{1,0:T(8,128)(2,1)} copy(bf16[16,4096]{1,0:T(8,128)(2,1)} %shard_map.64) | data formatting | bytes 262144

commit v4 on v3

--- a/solution.py
+++ b/solution.py
@@ -15,7 +15,7 @@
 CHUNKS = 4
 WINDOW = 3
 REDUCE_AT = 1.1
-LINE_STEP = 1.01
+LINE_STEP = 1.95
 
 
 def tables(local_rows, block_tokens):

time: 52.7 us -> 52 us (0.987)
  Pallas kernels: 51 us -> 50.3 us
    pallas_call x1, Pallas kernels: 51 us -> 50.3 us  [local_kernel(): pl.pallas_call(functools.partial(kernel, pairs, chunks), out_shape=jax.Sh...]
where the time goes in v4:
time: 52 us; the launch traced here: 51.9 us
  Pallas kernels  50.3 us (97%)
  local copies, waits for them, and re-layouts  1.57 us (3%)
    pallas_call x1, Pallas kernels, local_kernel(): pl.pallas_call(functools.partial(kernel, pairs, chunks), out_shape=jax.Sh...  50.3 us
    unnamed x1, local copies, waits for them, and re-layouts  1.57 us

profile of v4, /device:TPU:1, one launch (start us, length us, event | category | flops | bytes accessed | tf_op | source)
XLA Modules:
  0.0 51.9 jit_solution(78122599439104938)
XLA Ops:
  0.0 50.3 %shard_map.64 = bf16[16,4096]{1,0:T(8,128)(2,1)} custom-call(bf16[256,2048]{1,0:T(8,128)(2,1)} %hist_ref.1, bf16[256,2048]{1,0:T(8,128)(2,1)} %taps_ref.1, bf16[32,2048]{1,0:T(8,128)(2,1)} %gate_ref.1, bf16[2048,512]{1,0:T(8,128)(2,1)} %weight_ref.1, bf16[512,512]{1,0:T(8,128)(2,1)} %constant.6.fwd_ref, bf16[256,512]{1,0:T(8,128)(2,1)} %constant.7.inv_ref), custom_call_target="tpu_custom_call" | custom-call | tf_op jit(solution)/shard_map/pallas_call | solution.py:433
  50.3 1.6 %copy.8 = bf16[16,4096]{1,0:T(8,128)(2,1)} copy(bf16[16,4096]{1,0:T(8,128)(2,1)} %shard_map.64) | data formatting | bytes 262144
